TPU v7x, 32 devices: a whole 2x2x4 slice. The times are simulated.
32 devices in a mesh: row: 4 (over y, x), col: 8 (over z, core).
Axes of the slice: x: 2, y: 2, z: 4, core: 2. Of those that a mesh axis runs over, the one named last changes fastest.
Arguments:
- anc_inverse: float32 [10240, 10240], P('row', 'col'), may hold values from -0.0625 to 0.0625
- lower_anc: float32 [10240, 3, 384], P('col', None, 'row'), may hold values from -1.5 to 1.5
- upper_anc: float32 [10240, 3, 384], P('row', None, 'col'), may hold values from -0.75 to 0.75
- lower_edge: float32 [2, 384, 384], replicated, may hold values from -0.3125 to 0.3125
- upper_edge: float32 [2, 384, 384], replicated, may hold values from -0.3125 to 0.3125
- diag_inverse: float32 [3, 384, 384], replicated, may hold values from -6 to 6
- tile_mask: int32 [3, 80, 3], replicated, may hold values 0 or 1
Outputs:
- x_blocks: float32 [10240, 3, 384], P(('row', 'col'))
- y_blocks: float32 [8, 4, 320, 3, 384], P('col', 'row')
- z_blocks: float32 [3, 384, 384], P(None, 'row', 'col')
- cross_blocks: float32 [2, 2, 384, 384], P(None, None, 'row', 'col')
All inputs are finite; a program needn't handle non-finite values.
Results may differ from a plain program's by a relative error of at most 0.0001.
Values sent between devices are 32-bit elements; how exact they have to be, the bound alone decides.
A program may use at most 128 MiB of HBM per device.

v0:
```python
import jax
import jax.numpy as jnp
from jax import lax
from jax.sharding import PartitionSpec as P

W = 384
BLK = 128
SUPER = 3
precise = lax.Precision.HIGHEST


def product(left, right):
    return jnp.dot(left, right, precision=precise, preferred_element_type=jnp.float32)


def inner_product(left, right):
    return lax.dot_general(
        left, right, (((0,), (0,)), ((), ())), precision=precise, preferred_element_type=jnp.float32
    )


def outer_product(left, right):
    return lax.dot_general(
        left, right, (((1,), (1,)), ((), ())), precision=precise, preferred_element_type=jnp.float32
    )


def tile_pattern(tile_mask, first_block, blocks):
    window = lax.dynamic_slice_in_dim(tile_mask, first_block, blocks, 1).astype(jnp.float32)
    window = jnp.transpose(window, (1, 0, 2))
    widened = jnp.broadcast_to(window[:, None, :, :, None], (blocks, BLK, SUPER, W // BLK, BLK))
    return widened.reshape(blocks * BLK, SUPER, W)


def row_term(anc_inverse, lower_cols):
    return product(anc_inverse, lower_cols)


def col_term(anc_inverse, upper_rows):
    return inner_product(anc_inverse, upper_rows)


def per_device(anc_inverse, lower_anc, upper_anc, lower_edge, upper_edge, diag_inverse, tile_mask):
    rows_here, cols_here = anc_inverse.shape
    slab_rows = rows_here // lax.axis_size("col")
    row_index = lax.axis_index("row")
    col_index = lax.axis_index("col")
    col_pattern = tile_pattern(tile_mask, col_index * (cols_here // BLK), cols_here // BLK)
    row_pattern = tile_pattern(tile_mask, row_index * (rows_here // BLK), rows_here // BLK)
    lower_list = []
    upper_list = []
    cols_list = []
    rows_list = []
    lower_full = lax.all_gather(lower_anc, "row", axis=2, tiled=True) * col_pattern
    upper_full = lax.all_gather(upper_anc, "col", axis=2, tiled=True) * row_pattern
    cols_all = lax.psum_scatter(
        row_term(anc_inverse, lower_full.reshape(cols_here, SUPER * W)),
        "col",
        scatter_dimension=0,
        tiled=True,
    )
    rows_all = lax.psum_scatter(
        col_term(anc_inverse, upper_full.reshape(rows_here, SUPER * W)),
        "row",
        scatter_dimension=0,
        tiled=True,
    )
    cols_all = cols_all.reshape(slab_rows, SUPER, W)
    rows_all = rows_all.reshape(slab_rows, SUPER, W)
    for node_index in range(SUPER):
        lower_list.append(lower_full[:, node_index, :])
        upper_list.append(upper_full[:, node_index, :])
        cols_list.append(cols_all[:, node_index, :])
        rows_list.append(rows_all[:, node_index, :])
    x_list = []
    y_list = []
    corner_list = []
    cross_cols = []
    cross_rows = []
    for node_index in range(SUPER):
        lower_cur = lower_list[node_index]
        upper_cur = upper_list[node_index]
        inv_cols = -cols_list[node_index]
        inv_rows = -rows_list[node_index]
        upper_mine = lax.dynamic_slice_in_dim(upper_cur, col_index * slab_rows, slab_rows, 0)
        if node_index > 0:
            lower_side = lower_edge[node_index - 1]
            upper_side = upper_edge[node_index - 1]
            lower_mine = lax.dynamic_slice_in_dim(lower_cur, row_index * slab_rows, slab_rows, 0)
            rows_lower = inner_product(prev_rows, lower_mine)
            upper_cols = inner_product(upper_mine, prev_cols)
        if node_index > 0:
            rows_lower, upper_cols = lax.psum((rows_lower, upper_cols), ("row", "col"))
        if node_index > 0:
            cross_col = -(rows_lower + product(prev_corner, lower_side))
            cross_row = -(upper_cols + product(upper_side, prev_corner))
            inv_cols = inv_cols - product(prev_cols, lower_side)
            inv_rows = inv_rows - outer_product(prev_rows, upper_side)
            cross_cols.append(cross_col)
            cross_rows.append(cross_row)
        inv_corner = diag_inverse[node_index] - lax.psum(
            inner_product(upper_mine, inv_cols), ("row", "col")
        )
        if node_index > 0:
            inv_corner = inv_corner - product(upper_side, cross_col)
        x_list.append(inv_cols)
        y_list.append(inv_rows)
        corner_list.append(inv_corner)
        prev_cols = inv_cols
        prev_rows = inv_rows
        prev_corner = inv_corner
    x_blocks = jnp.stack(x_list, axis=1)
    y_blocks = jnp.stack(y_list, axis=1)[None, None]
    tile_rows = W // lax.axis_size("row")
    tile_cols = W // lax.axis_size("col")
    corners = jnp.stack(corner_list)
    corners = lax.dynamic_slice_in_dim(corners, row_index * tile_rows, tile_rows, 1)
    z_blocks = lax.dynamic_slice_in_dim(corners, col_index * tile_cols, tile_cols, 2)
    crossed = jnp.stack([jnp.stack(cross_cols), jnp.stack(cross_rows)])
    crossed = lax.dynamic_slice_in_dim(crossed, row_index * tile_rows, tile_rows, 2)
    cross_blocks = lax.dynamic_slice_in_dim(crossed, col_index * tile_cols, tile_cols, 3)
    return (x_blocks, y_blocks, z_blocks, cross_blocks)


def solution(mesh):
    return jax.shard_map(
        per_device,
        mesh=mesh,
        in_specs=(
            P("row", "col"),
            P("col", None, "row"),
            P("row", None, "col"),
            P(),
            P(),
            P(),
            P(),
        ),
        out_specs=(
            P(("row", "col"), None, None),
            P("col", "row", None, None, None),
            P(None, "row", "col"),
            P(None, None, "row", "col"),
        ),
        check_vma=False,
    )
```

profile of v0, /device:TPU:0, one launch (start us, length us, event | category | flops | bytes accessed | tf_op | source)
XLA Modules:
  0.0 565.6 jit_solution(17613502817447202190)
XLA Ops:
  8.9 4.2 broadcast_in_dim.6
  13.1 10.5 %reshape.42 = f32[1280,3,384]{2,0,1:T(8,128)} reshape(f32[10,128,3,3,128]{4,3,1,0,2:T(4,128)} %broadcast_in_dim.6) | data formatting | bytes 11796480 | tf_op jit(solution)/shard_map/reshape | solution.py:32
  23.6 55.8 %all-gather.3.cloned.1.call-done = f32[1280,3,384]{0,2,1:T(8,128)} async-done(((f32[1280,3,96]{0,2,1:T(8,128)}), f32[1280,3,384]{0,2,1:T(8,128)}) %all-gather.3.cloned.1.call-update) | async-done | bytes 5898256 | tf_op jit(solution)/shard_map/all_gather | solution.py:54
  79.3 7.7 %copy.70 = f32[1280,3,384]{2,0,1:T(8,128)} copy(f32[1280,3,384]{0,2,1:T(8,128)} %all-gather.3.cloned.1.call-done) | data formatting | bytes 11796480 | tf_op jit(solution)/shard_map/all_gather | solution.py:54
  87.0 9.3 %mul.30 = f32[1280,3,384]{2,0,1:T(8,128)} multiply(f32[1280,3,384]{2,0,1:T(8,128)} %copy.70, f32[1280,3,384]{2,0,1:T(8,128)} %reshape.42) | non-fusion elementwise | flops 1474560 | bytes 17694720 | tf_op jit(solution)/shard_map/mul | solution.py:54
  96.3 7.8 %copy.71 = f32[1280,3,384]{0,2,1:T(8,128)} copy(f32[1280,3,384]{2,0,1:T(8,128)} %mul.30) | data formatting | bytes 11796480 | tf_op jit(solution)/shard_map/mul | solution.py:54
  104.0 52.7 %convolution_bitcast_fusion = f32[2560,1152]{0,1:T(8,128)} fusion(f32[1280,1152]{0,1:T(8,128)} %bitcast.163, f32[2560,1280]{1,0:T(8,128)} %param.7), kind=kOutput, calls=%fused_computation | convolution fusion | flops 45298483200 | bytes 30801920 | tf_op jit(solution)/shard_map/dot_general | solution.py:13
  156.8 13.6 %copy.92 = f32[2560,1152]{1,0:T(8,128)} copy(f32[2560,1152]{0,1:T(8,128)} %convolution_bitcast_fusion) | data formatting | bytes 23592960
  171.1 6.0 %broadcast_in_dim.7 = f32[20,128,3,3,128]{1,0,4,3,2:T(8,128)} broadcast(f32[20,3,3]{0,2,1:T(4,128)S(1)} %convert_bitcast_fusion), dimensions={0,2,3} | broadcast | bytes 11797200 | tf_op jit(solution)/shard_map/broadcast_in_dim | solution.py:31
  177.1 13.7 %reshape.45 = f32[2560,3,384]{0,2,1:T(8,128)} reshape(f32[20,128,3,3,128]{1,0,4,3,2:T(8,128)} %broadcast_in_dim.7) | data formatting | bytes 23592960 | tf_op jit(solution)/shard_map/reshape | solution.py:32
  191.2 9.7 %mul.32 = f32[2560,3,384]{0,2,1:T(8,128)S(1)} multiply(f32[2560,3,384]{0,2,1:T(8,128)} %all-gather.5.cloned.1.call-done, f32[2560,3,384]{0,2,1:T(8,128)} %reshape.45) | non-fusion elementwise | flops 2949120 | bytes 35389440 | tf_op jit(solution)/shard_map/mul | solution.py:55
  200.9 4.3 copy-done
  205.3 50.1 %convolution_bitcast_fusion.1 = f32[1280,1152]{0,1:T(8,128)} fusion(f32[2560,1152]{0,1:T(8,128)S(1)} %bitcast.157, f32[2560,1280]{1,0:T(8,128)} %param.7), kind=kOutput, calls=%fused_computation.1 | convolution fusion | flops 45298483200 | bytes 30801920 | tf_op jit(solution)/shard_map/dot_general | solution.py:17
  255.4 7.7 %copy.94 = f32[1280,1152]{1,0:T(8,128)} copy(f32[1280,1152]{0,1:T(8,128)} %convolution_bitcast_fusion.1) | data formatting | bytes 11796480
  263.3 4.3 fusion.75
  267.6 9.3 %fusion.74 = (f32[2560,1,384]{0,2,1:T(8,128)}, f32[2560,1,384]{0,2,1:T(8,128)}, f32[2560,1,384]{0,2,1:T(8,128)}) fusion(f32[2560,3,384]{0,2,1:T(8,128)} %copy-done), kind=kLoop, calls=%fused_computation.100 | loop fusion | bytes 23592960 | tf_op jit(solution)/shard_map/slice | solution.py:72
  276.9 36.6 %reduce-scatter.7.cloned.1.call-done = f32[320,1152]{1,0:T(8,128)} async-done(((f32[2560,1152]{1,0:T(8,128)}), f32[320,1152]{1,0:T(8,128)}) %reduce-scatter.7.cloned.1.call-update) | async-done | bytes 1474576
  319.1 3.3 fusion.16
  323.5 3.3 fusion.18
  326.7 3.3 fusion.12
  331.9 3.2 fusion.14
  335.1 46.5 %reduce-scatter.9.cloned.1.call-done = f32[320,1152]{1,0:T(8,128)} async-done(((f32[1280,1152]{1,0:T(8,128)}), f32[320,1152]{1,0:T(8,128)}) %reduce-scatter.9.cloned.1.call-update) | async-done | bytes 1474576
  388.7 3.3 fusion.20
  407.0 137.7 %all-reduce.3.cloned.1.call-done = (f32[384,384]{1,0:T(8,128)}, f32[384,384]{1,0:T(8,128)}, f32[384,384]{1,0:T(8,128)}, f32[384,384]{1,0:T(8,128)}, f32[384,384]...) async-done(((f32[384,384]{1,0:T(8,128)}, f32[384,384]{1,0:T(8,128)}, f32[384,384]{1,0:T(8,128)}, f32[384,384]{1,0:T(8,128)}, f32[384,384]{1,0:T(8,128)}, ...) | async-done | bytes 4128784 | tf_op jit(solution)/shard_map/psum | solution.py:101
  (79 shorter events, 47.5 us)
Async XLA Ops:
  7.2 1.5 copy-start.16
  7.2 72.2 %all-gather.3.cloned.1.call-start = ((), (), s32[]{:S(2)}) async-start(), calls=%async_computation.2 | async-start | bytes 7372800 | tf_op jit(solution)/shard_map/all_gather | solution.py:54
  7.9 183.3 %all-gather.5.cloned.1.call-start = ((), (), s32[]{:S(2)}) async-start(), calls=%async_computation.3 | async-start | bytes 13271040 | tf_op jit(solution)/shard_map/all_gather | solution.py:55
  8.7 304.8 %reduce-scatter.7.cloned.1.call-start = ((), (), s32[]{:S(2)}) async-start(), calls=%async_computation.4 | async-start | bytes 13271040
  170.4 211.2 %reduce-scatter.9.cloned.1.call-start = ((), (), s32[]{:S(2)}) async-start(), calls=%async_computation.5 | async-start | bytes 7372800
  200.9 4.3 copy-start
  263.1 281.6 %all-reduce.3.cloned.1.call-start = ((), (), s32[]{:S(2)}) async-start(), calls=%async_computation.6 | async-start | bytes 8257536 | tf_op jit(solution)/shard_map/psum | solution.py:101
  317.8 4.5 copy-start.4
  319.1 3.3 copy-start.9
  331.1 0.8 copy-start.6
  385.2 6.8 %copy-start.1 = (f32[2,384,384]{2,1,0:T(8,128)S(1)}, f32[2,384,384]{2,1,0:T(8,128)}, u32[]{:S(2)}) copy-start(f32[2,384,384]{2,1,0:T(8,128)} %param.11) | copy-start | bytes 3538948
  388.7 3.3 copy-start.10
  400.4 2.1 copy-start.7
  404.7 1.1 copy-start.8
  544.7 1.5 copy-start.2
  544.7 1.6 copy-start.15
  544.7 4.2 copy-start.14
  546.1 2.7 copy-start.3
  546.1 2.7 copy-start.5
  548.8 1.3 copy-start.13
  550.1 1.3 copy-start.12
  551.5 1.6 copy-start.11
Sparse Core Ops, SparseCore 0:
  9.8 69.4 all-gather.2
  81.0 110.1 all-gather.4
  193.5 119.9 reduce-scatter.6
  316.4 65.2 reduce-scatter.8
  399.6 144.9 all-reduce.2
where the time goes:
time: 574 us; the launch traced here: 566 us
  waiting for transfers between devices  278 us (48%)
  matrix products  140 us (24%)
  local copies, waits for them, and re-layouts  105 us (18%)
  other arithmetic  26.1 us (5%)
  between operations  14.4 us (3%)
    psum x1, waiting for transfers between devices, per_device(): lax.psum(inner_product(upper_mine, inv_cols), ('row', 'col'))  138 us
    unnamed x7, waiting for transfers between devices  84.6 us
    dot_general x8, matrix products, inner_product(): lax.dot_general(left, right, (((0,), (0,)), ((), ())), precision=precise,...  72.9 us
    dot_general x9, matrix products, product(): jnp.dot(left, right, precision=precise, preferred_element_type=jnp.float32)  65.3 us
    all_gather x1, waiting for transfers between devices, per_device(): lax.all_gather(lower_anc, 'row', axis=2, tiled=True) * col_pattern  55.8 us
    unnamed x46, local copies, waits for them, and re-layouts  39.8 us
    reshape x2, local copies, waits for them, and re-layouts, tile_pattern(): return widened.reshape(blocks * BLK, SUPER, W)  24.2 us
  transfers between devices with their start and end apart: 5, of which 5 were waited for; matrix products, arithmetic and copies ran while one was open for 42% of the time, Pallas kernels for 0%

commit v1 on v0

--- a/solution.py
+++ b/solution.py
@@ -98,8 +98,8 @@
             inv_rows = inv_rows - outer_product(prev_rows, upper_side)
             cross_cols.append(cross_col)
             cross_rows.append(cross_row)
-        inv_corner = diag_inverse[node_index] - lax.psum(
-            inner_product(upper_mine, inv_cols), ("row", "col")
+        inv_corner = diag_inverse[node_index] - jnp.sum(
+            lax.all_gather(inner_product(upper_mine, inv_cols), ("row", "col")), axis=0
         )
         if node_index > 0:
             inv_corner = inv_corner - product(upper_side, cross_col)

time: 574 us -> 930 us (1.62)
  waiting for transfers between devices: 278 us -> 596 us
  other arithmetic: 26.1 us -> 49.4 us
  local copies, waits for them, and re-layouts: 105 us -> 117 us
    all_gather x0 -> x3, waiting for transfers between devices: none -> 313 us  [per_device(): lax.all_gather(inner_product(upper_mine, inv_cols), ('row', 'col'))]
    reduce_sum x0 -> x3, other arithmetic: none -> 22.6 us  [per_device(): jnp.sum(lax.all_gather(inner_product(upper_mine, inv_cols), ('row', 'col'...]
    unnamed x7 -> x10, waiting for transfers between devices: 84.6 us -> 94.6 us
    unnamed x46 -> x44, local copies, waits for them, and re-layouts: 39.8 us -> 44.9 us
  transfers between devices with their start and end apart: 5 -> 8, of which waited for: 5 -> 8; matrix products, arithmetic and copies ran while one was open for 42% -> 32% of each run, Pallas kernels for 0% -> 0%
where the time goes in v1:
time: 930 us; the launch traced here: 922 us
  waiting for transfers between devices  596 us (64%)
  matrix products  143 us (15%)
  local copies, waits for them, and re-layouts  117 us (13%)
  other arithmetic  49.4 us (5%)
  between operations  14.7 us (2%)
    all_gather x3, waiting for transfers between devices, per_device(): lax.all_gather(inner_product(upper_mine, inv_cols), ('row', 'col'))  313 us
    psum x1, waiting for transfers between devices, per_device(): rows_lower, upper_cols = lax.psum((rows_lower, upper_cols), ('row', 'col'))  131 us
    unnamed x10, waiting for transfers between devices  94.6 us
    dot_general x8, matrix products, inner_product(): lax.dot_general(left, right, (((0,), (0,)), ((), ())), precision=precise,...  73 us
    dot_general x9, matrix products, product(): jnp.dot(left, right, precision=precise, preferred_element_type=jnp.float32)  68.1 us
    all_gather x1, waiting for transfers between devices, per_device(): lax.all_gather(lower_anc, 'row', axis=2, tiled=True) * col_pattern  55.8 us
    unnamed x44, local copies, waits for them, and re-layouts  44.9 us
    reshape x2, local copies, waits for them, and re-layouts, tile_pattern(): return widened.reshape(blocks * BLK, SUPER, W)  24.1 us
  transfers between devices with their start and end apart: 8, of which 8 were waited for; matrix products, arithmetic and copies ran while one was open for 32% of the time, Pallas kernels for 0%

profile of v1, /device:TPU:0, one launch (start us, length us, event | category | flops | bytes accessed | tf_op | source)
XLA Modules:
  0.0 921.8 jit_solution(4696724931748309982)
XLA Ops:
  13.0 10.5 %reshape.47 = f32[1280,3,384]{2,0,1:T(8,128)} reshape(f32[10,128,3,3,128]{4,3,1,0,2:T(4,128)} %broadcast_in_dim.6) | data formatting | bytes 11796480 | tf_op jit(solution)/shard_map/reshape | solution.py:32
  23.5 55.8 %all-gather.9.cloned.1.call-done = f32[1280,3,384]{0,2,1:T(8,128)} async-done(((f32[1280,3,96]{0,2,1:T(8,128)}), f32[1280,3,384]{0,2,1:T(8,128)}) %all-gather.9.cloned.1.call-update) | async-done | bytes 5898256 | tf_op jit(solution)/shard_map/all_gather | solution.py:54
  79.3 7.7 copy.73
  87.0 9.3 %mul.30 = f32[1280,3,384]{2,0,1:T(8,128)} multiply(f32[1280,3,384]{2,0,1:T(8,128)} %copy.73, f32[1280,3,384]{2,0,1:T(8,128)} %reshape.47) | non-fusion elementwise | flops 1474560 | bytes 17694720 | tf_op jit(solution)/shard_map/mul | solution.py:54
  96.3 7.8 copy.74
  104.1 52.6 %convolution_bitcast_fusion = f32[2560,1152]{0,1:T(8,128)} fusion(f32[1280,1152]{0,1:T(8,128)} %bitcast.168, f32[2560,1280]{1,0:T(8,128)} %param.7), kind=kOutput, calls=%fused_computation | convolution fusion | flops 45298483200 | bytes 30801920 | tf_op jit(solution)/shard_map/dot_general | solution.py:13
  156.7 13.5 %copy.96 = f32[2560,1152]{1,0:T(8,128)} copy(f32[2560,1152]{0,1:T(8,128)} %convolution_bitcast_fusion) | data formatting | bytes 23592960
  170.6 6.0 broadcast_in_dim.7
  176.6 13.7 %reshape.50 = f32[2560,3,384]{0,2,1:T(8,128)} reshape(f32[20,128,3,3,128]{1,0,4,3,2:T(8,128)} %broadcast_in_dim.7) | data formatting | bytes 23592960 | tf_op jit(solution)/shard_map/reshape | solution.py:32
  191.2 9.7 %mul.32 = f32[2560,3,384]{0,2,1:T(8,128)S(1)} multiply(f32[2560,3,384]{0,2,1:T(8,128)} %all-gather.11.cloned.1.call-done, f32[2560,3,384]{0,2,1:T(8,128)} %reshape.50) | non-fusion elementwise | flops 2949120 | bytes 35389440 | tf_op jit(solution)/shard_map/mul | solution.py:55
  200.9 4.3 copy-done
  205.3 50.0 %convolution_bitcast_fusion.1 = f32[1280,1152]{0,1:T(8,128)} fusion(f32[2560,1152]{0,1:T(8,128)S(1)} %bitcast.159, f32[2560,1280]{1,0:T(8,128)} %param.7), kind=kOutput, calls=%fused_computation.1 | convolution fusion | flops 45298483200 | bytes 30801920 | tf_op jit(solution)/shard_map/dot_general | solution.py:17
  255.3 7.7 copy.98
  263.5 9.2 %fusion.75 = (f32[2560,1,384]{0,2,1:T(8,128)}, f32[2560,1,384]{0,2,1:T(8,128)}, f32[2560,1,384]{0,2,1:T(8,128)}) fusion(f32[2560,3,384]{0,2,1:T(8,128)} %copy-done), kind=kLoop, calls=%fused_computation.101 | loop fusion | bytes 23592960 | tf_op jit(solution)/shard_map/slice | solution.py:72
  272.7 40.8 %reduce-scatter.7.cloned.1.call-done = f32[320,1152]{1,0:T(8,128)} async-done(((f32[2560,1152]{1,0:T(8,128)}), f32[320,1152]{1,0:T(8,128)}) %reduce-scatter.7.cloned.1.call-update) | async-done | bytes 1474576
  324.9 4.3 fusion.76
  329.2 52.4 %reduce-scatter.9.cloned.1.call-done = f32[320,1152]{1,0:T(8,128)} async-done(((f32[1280,1152]{1,0:T(8,128)}), f32[320,1152]{1,0:T(8,128)}) %reduce-scatter.9.cloned.1.call-update) | async-done | bytes 1474576
  427.8 80.8 %all-gather.13.cloned.1.call-done = f32[12288,384]{1,0:T(8,128)} async-done(((f32[384,384]{1,0:T(8,128)}), f32[12288,384]{1,0:T(8,128)}) %all-gather.13.cloned.1.call-update) | async-done | bytes 18874384 | tf_op jit(solution)/shard_map/all_gather | solution.py:102
  508.5 7.3 reduce_sum.29
  516.9 116.8 %all-gather.15.cloned.1.call-done = f32[12288,384]{1,0:T(8,128)} async-done(((f32[384,384]{1,0:T(8,128)}), f32[12288,384]{1,0:T(8,128)}) %all-gather.15.cloned.1.call-update) | async-done | bytes 18874384 | tf_op jit(solution)/shard_map/all_gather | solution.py:102
  633.7 7.3 reduce_sum.31
  643.4 131.2 %all-reduce.3.cloned.1.call-done = (f32[384,384]{1,0:T(8,128)}, f32[384,384]{1,0:T(8,128)}, f32[384,384]{1,0:T(8,128)}, f32[384,384]{1,0:T(8,128)}) async-done(((f32[384,384]{1,0:T(8,128)}, f32[384,384]{1,0:T(8,128)}, f32[384,384]{1,0:T(8,128)}, f32[384,384]{1,0:T(8,128)}), (f32[384,384]{1,0:T(8,128)}, f32[384,384]{1,0:T(8,128)}, f32[384,384]{1,0:T(8,128)}, ...) | async-done | bytes 2359312 | tf_op jit(solution)/shard_map/psum | solution.py:93
  784.6 115.8 %all-gather.17.cloned.1.call-done = f32[12288,384]{1,0:T(8,128)} async-done(((f32[384,384]{1,0:T(8,128)}), f32[12288,384]{1,0:T(8,128)}) %all-gather.17.cloned.1.call-update) | async-done | bytes 18874384 | tf_op jit(solution)/shard_map/all_gather | solution.py:102
  900.5 8.1 reduce_sum.32
  (93 shorter events, 84.5 us)
Async XLA Ops:
  7.2 1.5 copy-start.14
  7.2 72.2 %all-gather.9.cloned.1.call-start = ((), (), s32[]{:S(2)}) async-start(), calls=%async_computation.2 | async-start | bytes 7372800 | tf_op jit(solution)/shard_map/all_gather | solution.py:54
  7.9 183.3 %all-gather.11.cloned.1.call-start = ((), (), s32[]{:S(2)}) async-start(), calls=%async_computation.3 | async-start | bytes 13271040 | tf_op jit(solution)/shard_map/all_gather | solution.py:55
  8.7 304.8 %reduce-scatter.7.cloned.1.call-start = ((), (), s32[]{:S(2)}) async-start(), calls=%async_computation.7 | async-start | bytes 13271040
  170.2 211.4 %reduce-scatter.9.cloned.1.call-start = ((), (), s32[]{:S(2)}) async-start(), calls=%async_computation.8 | async-start | bytes 7372800
  200.9 4.3 copy-start
  263.0 245.5 %all-gather.13.cloned.1.call-start = ((), (), s32[]{:S(2)}) async-start(), calls=%async_computation.4 | async-start | bytes 19464192 | tf_op jit(solution)/shard_map/all_gather | solution.py:102
  316.6 3.9 copy-start.2
  320.2 313.5 %all-gather.15.cloned.1.call-start = ((), (), s32[]{:S(2)}) async-start(), calls=%async_computation.5 | async-start | bytes 19464192 | tf_op jit(solution)/shard_map/all_gather | solution.py:102
  324.9 449.7 %all-reduce.3.cloned.1.call-start = ((), (), s32[]{:S(2)}) async-start(), calls=%async_computation.9 | async-start | bytes 4718592 | tf_op jit(solution)/shard_map/psum | solution.py:93
  391.6 6.6 copy-start.1
  391.6 6.6 copy-start.10
  402.5 498.0 %all-gather.17.cloned.1.call-start = ((), (), s32[]{:S(2)}) async-start(), calls=%async_computation.6 | async-start | bytes 19464192 | tf_op jit(solution)/shard_map/all_gather | solution.py:102
  407.1 0.8 copy-start.5
  421.0 2.1 copy-start.6
  423.1 3.4 copy-start.9
  642.0 135.1 %copy-start.3 = (f32[2,384,384]{2,1,0:T(8,128)S(1)}, f32[2,384,384]{2,1,0:T(8,128)}, u32[]{:S(2)}) copy-start(f32[2,384,384]{2,1,0:T(8,128)} %param.10) | copy-start | bytes 3538948
  774.6 2.5 copy-start.13
  774.6 3.9 copy-start.7
  774.6 3.9 copy-start.8
  778.5 2.1 copy-start.12
  778.5 3.7 copy-start.4
  778.5 3.7 copy-start.11
Sparse Core Ops, SparseCore 0:
  9.8 69.4 all-gather.8
  81.0 110.1 all-gather.10
  193.5 119.9 reduce-scatter.6
  316.4 65.2 reduce-scatter.8
  384.5 123.9 all-gather.12
  511.4 122.2 all-gather.14
  639.7 134.8 all-reduce.2
  777.6 122.7 all-gather.16
